TPU v7x, 512 devices: a whole 4x8x8 slice. The times are simulated.
512 devices in a mesh: doc: 16 (over z, core), gram: 32 (over x, y).
Axes of the slice: x: 4, y: 8, z: 8, core: 2. Of those that a mesh axis runs over, the one named last changes fastest.
Arguments:
- w_factor: bfloat16 [24576, 256], P(('doc', 'gram')), may hold values from 0.003 to 0.1
- h_factor: bfloat16 [49152, 256], P(('gram', 'doc')), may hold values from 0.003 to 0.1
- tile_counts: bfloat16 [16, 32, 24, 128, 128], P('doc', 'gram'), may hold values from 0 to 30, as said below
- tile_rows: int32 [16, 32, 24], P('doc', 'gram'), may hold values from 0 to 11, as said below
- tile_cols: int32 [16, 32, 24], P('doc', 'gram'), may hold values from 0 to 11, as said below
- tile_live: int32 [16, 32], P('doc', 'gram'), may hold values from 1 to 24, as said below
Outputs:
- w_next: bfloat16 [24576, 256], P(('doc', 'gram'))
- h_next: bfloat16 [49152, 256], P(('gram', 'doc'))
Inputs may be any that keep to these rules, and one draw needn't show every extreme that they name: `tile_rows`: within one device pair the first tile_live slots name distinct tiles; slots hold positions in every case. `tile_cols`: see tile_rows. `tile_live`: some device pair holds 24 tiles. `tile_counts`: whole numbers.
All inputs are finite; a program needn't handle non-finite values.
Results may differ from a plain program's by a relative error of at most 0.0021.
Values may be sent and summed in bfloat16 or wider, within the bound.
A program may use at most 64 MiB of HBM per device.

v0:
```python
import jax
import jax.numpy as jnp
from jax import lax
from jax.sharding import PartitionSpec as P

GROUP = 8


def group_terms(w_tiles, h_tiles, rows, cols, counts, keep):
    wt = jnp.take(w_tiles, rows, axis=0)
    ht = jnp.take(h_tiles, cols, axis=0)
    model = jnp.einsum("spk,sqk->spq", wt, ht, preferred_element_type=jnp.float32)
    ratio = (counts.astype(jnp.float32) / model * keep[:, None, None]).astype(jnp.bfloat16)
    w_part = jnp.einsum("spq,sqk->spk", ratio, ht, preferred_element_type=jnp.float32)
    h_part = jnp.einsum("spq,spk->sqk", ratio, wt, preferred_element_type=jnp.float32)
    pick_r = (rows[:, None] == jnp.arange(w_tiles.shape[0], dtype=jnp.int32)[None, :]).astype(
        jnp.float32
    )
    pick_c = (cols[:, None] == jnp.arange(h_tiles.shape[0], dtype=jnp.int32)[None, :]).astype(
        jnp.float32
    )
    add_w = jnp.einsum("st,spk->tpk", pick_r, w_part, precision=lax.Precision.HIGHEST)
    add_h = jnp.einsum("st,spk->tpk", pick_c, h_part, precision=lax.Precision.HIGHEST)
    return (add_w, add_h)


def body(w_factor, h_factor, tile_counts, tile_rows, tile_cols, tile_live):
    topics = w_factor.shape[1]
    w_block = lax.all_gather(w_factor, "gram", axis=0, tiled=True)
    h_block = lax.all_gather(h_factor, "doc", axis=0, tiled=True)
    tile_side = tile_counts.shape[3]
    w_tiles = w_block.reshape(-1, tile_side, topics)
    h_tiles = h_block.reshape(-1, tile_side, topics)
    rows = tile_rows[0, 0]
    cols = tile_cols[0, 0]
    counts = tile_counts[0, 0]
    live = tile_live[0, 0]
    slots = rows.shape[0]
    width = GROUP
    start = (jnp.zeros(w_tiles.shape, jnp.float32), jnp.zeros(h_tiles.shape, jnp.float32))
    steps = slots // width
    marks = (jnp.arange(slots, dtype=jnp.int32) < live).astype(jnp.float32)

    def visit(carry, pieces):
        part_rows, part_cols, part_counts, part_keep = pieces
        add_w, add_h = group_terms(w_tiles, h_tiles, part_rows, part_cols, part_counts, part_keep)
        return ((carry[0] + add_w, carry[1] + add_h), None)

    pieces = (
        rows.reshape(steps, width),
        cols.reshape(steps, width),
        counts.reshape(steps, width, tile_side, tile_side),
        marks.reshape(steps, width),
    )
    (w_numer, h_numer), _ = lax.scan(visit, start, pieces)
    flat_w = w_numer.reshape(-1, topics)
    flat_h = h_numer.reshape(-1, topics)
    w_rows = w_factor.shape[0]
    h_rows = h_factor.shape[0]
    summed_w = lax.psum(flat_w, "gram")
    share_w = lax.dynamic_slice_in_dim(summed_w, lax.axis_index("gram") * w_rows, w_rows, 0)
    summed_h = lax.psum(flat_h, "doc")
    share_h = lax.dynamic_slice_in_dim(summed_h, lax.axis_index("doc") * h_rows, h_rows, 0)
    h_sums = jnp.sum(h_factor.astype(jnp.float32), axis=0)
    w_sums = jnp.sum(w_factor.astype(jnp.float32), axis=0)
    w_denom, h_denom = lax.psum((h_sums, w_sums), ("doc", "gram"))
    w_next = (w_factor.astype(jnp.float32) * share_w / w_denom).astype(jnp.bfloat16)
    h_next = (h_factor.astype(jnp.float32) * share_h / h_denom).astype(jnp.bfloat16)
    return (w_next, h_next)


def solution(mesh):
    in_specs = (
        P(("doc", "gram"), None),
        P(("gram", "doc"), None),
        P("doc", "gram", None, None, None),
        P("doc", "gram", None),
        P("doc", "gram", None),
        P("doc", "gram"),
    )
    out_specs = (P(("doc", "gram"), None), P(("gram", "doc"), None))
    return jax.shard_map(body, mesh=mesh, in_specs=in_specs, out_specs=out_specs, check_vma=False)
```

profile of v0, /device:TPU:64, one launch (start us, length us, event | category | flops | bytes accessed | tf_op | source)
XLA Modules:
  0.0 419.8 jit_solution(2480098275050584792)
XLA Ops:
  7.2 0.0 all-reduce.6.cloned.1.call-start
  7.2 0.5 broadcast.73
  7.7 1.3 reduce.6
  9.1 0.1 reshape_squeeze.9
  9.1 50.8 %all_gather.6 = bf16[1536,256]{1,0:T(8,128)(2,1)S(1)} all-gather(bf16[48,256]{1,0:T(8,128)(2,1)} %param.10), channel_id=1, replica_groups=mesh['doc'=16,'gram'=32] {'gram'}, dimensions={0}, use_global_device_ids=true | all-gather | bytes 811008 | tf_op jit(solution)/shard_map/all_gather | solution.py:29
  60.0 1.3 reduce.7
  61.3 0.1 reshape_squeeze.11
  61.4 23.9 %all_gather.7 = bf16[1536,256]{1,0:T(8,128)(2,1)} all-gather(bf16[96,256]{1,0:T(8,128)(2,1)} %param.11), channel_id=1, replica_groups=mesh['doc'=16,'gram'=32] {'doc'}, dimensions={0}, use_global_device_ids=true | all-gather | bytes 835584 | tf_op jit(solution)/shard_map/all_gather | solution.py:30
  85.9 38.7 %while.13 = (s32[]{:T(128)}, f32[12,128,256]{2,0,1:T(8,128)S(1)}, f32[12,128,256]{2,0,1:T(8,128)}, s32[3,8]{1,0:T(4,128)S(1)}, bf16[3,8,128,128]{3,2,1,0:T(8,128...) while((s32[]{:T(128)}, f32[12,128,256]{2,0,1:T(8,128)S(1)}, ...), condition=%wide.region_1.3_spmd.clone, body=%wide.region_0.2_spmd.clone.sunk | while | flops 279972160 | bytes 40903584 | solution.py:55
  85.9 0.0 copy-start.5
  86.0 0.6 gather_fusion
  86.6 0.0 copy-start.2
  86.6 0.2 copy-done.5
  86.8 1.7 gather_fusion.1
  88.5 0.0 copy-start.4
  88.6 0.0 copy-done.2
  88.6 0.8 copy-done.4
  89.3 1.3 fusion.44
  90.7 1.4 fusion.45
  92.1 0.0 copy-start.3
  92.1 0.0 copy-start
  92.1 2.5 select_add_fusion.4
  94.6 0.0 copy-done.3
  94.6 0.4 fusion.46
  95.0 0.0 copy-done
  95.0 0.0 copy-start.6
  95.0 2.5 select_add_fusion.5
  97.5 0.0 copy-start.1
  97.5 1.3 copy-done.1
  98.8 0.0 copy-done.6
  98.9 0.6 gather_fusion
  99.5 0.0 copy-start.2
  99.5 0.2 copy-done.5
  99.7 1.7 gather_fusion.1
  101.5 0.8 copy-done.4
  102.2 1.3 fusion.44
  103.6 1.4 fusion.45
  105.0 2.5 select_add_fusion.4
  107.5 0.4 fusion.46
  107.9 2.5 select_add_fusion.5
  110.4 1.3 copy-done.1
  111.8 0.6 gather_fusion
  112.4 0.2 copy-done.5
  112.6 1.7 gather_fusion.1
  114.4 0.8 copy-done.4
  115.1 1.3 fusion.44
  116.5 1.4 fusion.45
  117.9 2.5 select_add_fusion.4
  120.4 0.4 fusion.46
  120.8 2.5 select_add_fusion.5
  123.3 1.3 copy-done.1
  124.6 0.0 copy-done.6
  124.6 3.7 copy.9
  128.3 0.0 all-reduce.6.cloned.1.call-update
  128.3 0.0 all-reduce.4.cloned.1.call-start
  128.4 0.0 copy-start.8
  128.4 0.0 copy-start.7
  128.4 2.1 copy.8
  130.5 0.0 all-reduce.4.cloned.1.call-update
  130.6 96.5 %all-reduce = (f32[256]{0:T(256)S(1)}, f32[256]{0:T(256)S(1)}) all-reduce(f32[256]{0:T(256)S(1)} %convert_reduce_fusion, f32[256]{0:T(256)S(1)} %convert_reduce_fusion.1), channel_id=1, replica_groups=mesh['doc'=16,'gram'=32] {'doc','gram'}, use_global_device_ids=true, to_apply=%region_4.6 | all-reduce | flops 512 | bytes 4096 | tf_op jit(solution)/shard_map/psum | solution.py:66
  227.1 15.2 %all-reduce.6.cloned.1.call-done = f32[1536,256]{1,0:T(8,128)} async-done(((f32[1536,256]{1,0:T(8,128)}), f32[1536,256]{1,0:T(8,128)}) %all-reduce.6.cloned.1.call-update) | async-done | bytes 1572880 | tf_op jit(solution)/shard_map/psum | solution.py:62
  242.3 1.5 fusion.19
  243.8 167.7 %all-reduce.4.cloned.1.call-done = f32[1536,256]{1,0:T(8,128)} async-done(((f32[1536,256]{1,0:T(8,128)}), f32[1536,256]{1,0:T(8,128)}) %all-reduce.4.cloned.1.call-update) | async-done | bytes 1572880 | tf_op jit(solution)/shard_map/psum | solution.py:60
  411.6 1.4 fusion.21
  (45 shorter events, 0.2 us)
Async XLA Ops:
  7.2 235.2 %all-reduce.6.cloned.1.call-start = ((), (), s32[]{:S(2)}) async-start(), calls=%async_computation.1 | async-start | bytes 3145728 | tf_op jit(solution)/shard_map/psum | solution.py:62
  85.9 0.9 copy-start.5
  86.6 2.0 copy-start.2
  88.5 0.8 copy-start.4
  92.1 2.5 copy-start.3
  92.1 2.9 copy-start
  95.0 3.8 copy-start.6
  97.5 1.4 copy-start.1
  98.8 0.9 copy-start.5
  99.5 2.0 copy-start.2
  101.4 0.8 copy-start.4
  105.0 2.5 copy-start.3
  105.0 2.9 copy-start
  107.9 3.8 copy-start.6
  110.4 1.4 copy-start.1
  111.7 0.9 copy-start.5
  112.4 2.0 copy-start.2
  114.3 0.8 copy-start.4
  117.9 2.5 copy-start.3
  117.9 2.9 copy-start
  120.8 3.8 copy-start.6
  123.3 1.4 copy-start.1
  128.3 283.3 %all-reduce.4.cloned.1.call-start = ((), (), s32[]{:S(2)}) async-start(), calls=%async_computation | async-start | bytes 3145728 | tf_op jit(solution)/shard_map/psum | solution.py:60
  128.4 2.2 copy-start.8
  128.4 2.2 copy-start.7
Sparse Core Ops, SparseCore 0:
  128.4 113.8 all-reduce.5
  245.7 165.8 all-reduce.3
where the time goes:
time: 421 us; the launch traced here: 420 us
  waiting for transfers between devices  183 us (43%)
  blocking collectives  171 us (41%)
  matrix products  24.2 us (6%)
  local copies, waits for them, and re-layouts  20.4 us (5%)
  between operations  14.8 us (4%)
  other arithmetic  5.76 us (1%)
    psum x1, waiting for transfers between devices, body(): summed_w = lax.psum(flat_w, 'gram')  168 us
    psum x1, blocking collectives, body(): w_denom, h_denom = lax.psum((h_sums, w_sums), ('doc', 'gram'))  96.5 us
    all_gather x1, blocking collectives, body(): w_block = lax.all_gather(w_factor, 'gram', axis=0, tiled=True)  50.8 us
    all_gather x1, blocking collectives, body(): h_block = lax.all_gather(h_factor, 'doc', axis=0, tiled=True)  23.9 us
    psum x1, waiting for transfers between devices, body(): summed_h = lax.psum(flat_h, 'doc')  15.2 us
  transfers between devices with their start and end apart: 2, of which 2 were waited for; matrix products, arithmetic and copies ran while one was open for 1% of the time, Pallas kernels for 0%

commit v1 on v0

--- a/solution.py
+++ b/solution.py
@@ -63,7 +63,7 @@
     share_h = lax.dynamic_slice_in_dim(summed_h, lax.axis_index("doc") * h_rows, h_rows, 0)
     h_sums = jnp.sum(h_factor.astype(jnp.float32), axis=0)
     w_sums = jnp.sum(w_factor.astype(jnp.float32), axis=0)
-    w_denom, h_denom = lax.psum((h_sums, w_sums), ("doc", "gram"))
+    w_denom, h_denom = lax.psum(lax.psum((h_sums, w_sums), "doc"), "gram")
     w_next = (w_factor.astype(jnp.float32) * share_w / w_denom).astype(jnp.bfloat16)
     h_next = (h_factor.astype(jnp.float32) * share_h / h_denom).astype(jnp.bfloat16)
     return (w_next, h_next)

time: 421 us -> 421 us (level)
    psum x1 -> x2, blocking collectives: 96.5 us -> 95.4 us  [body(): w_denom, h_denom = lax.psum(lax.psum((h_sums, w_sums), 'doc'), 'gram')]
where the time goes in v1:
time: 421 us; the launch traced here: 420 us
  waiting for transfers between devices  184 us (44%)
  blocking collectives  170 us (40%)
  matrix products  24.2 us (6%)
  local copies, waits for them, and re-layouts  20.4 us (5%)
  between operations  14.8 us (4%)
  other arithmetic  5.75 us (1%)
    psum x1, waiting for transfers between devices, body(): summed_w = lax.psum(flat_w, 'gram')  168 us
    psum x2, blocking collectives, body(): w_denom, h_denom = lax.psum(lax.psum((h_sums, w_sums), 'doc'), 'gram')  95.4 us
    all_gather x1, blocking collectives, body(): w_block = lax.all_gather(w_factor, 'gram', axis=0, tiled=True)  50.8 us
    all_gather x1, blocking collectives, body(): h_block = lax.all_gather(h_factor, 'doc', axis=0, tiled=True)  23.9 us
    psum x1, waiting for transfers between devices, body(): summed_h = lax.psum(flat_h, 'doc')  16.6 us
  transfers between devices with their start and end apart: 2, of which 2 were waited for; matrix products, arithmetic and copies ran while one was open for 1% of the time, Pallas kernels for 0%

profile of v1, /device:TPU:64, one launch (start us, length us, event | category | flops | bytes accessed | tf_op | source)
XLA Modules:
  0.0 420.0 jit_solution(14159535712012497459)
XLA Ops:
  7.2 0.0 all-reduce.7.cloned.1.call-start
  7.2 0.5 broadcast.73
  7.7 1.3 reduce.6
  9.1 0.1 reshape_squeeze.9
  9.1 50.8 %all_gather.6 = bf16[1536,256]{1,0:T(8,128)(2,1)S(1)} all-gather(bf16[48,256]{1,0:T(8,128)(2,1)} %param.10), channel_id=1, replica_groups=mesh['doc'=16,'gram'=32] {'gram'}, dimensions={0}, use_global_device_ids=true | all-gather | bytes 811008 | tf_op jit(solution)/shard_map/all_gather | solution.py:29
  60.0 1.3 reduce.7
  61.3 0.1 reshape_squeeze.11
  61.4 23.9 %all_gather.7 = bf16[1536,256]{1,0:T(8,128)(2,1)} all-gather(bf16[96,256]{1,0:T(8,128)(2,1)} %param.11), channel_id=1, replica_groups=mesh['doc'=16,'gram'=32] {'doc'}, dimensions={0}, use_global_device_ids=true | all-gather | bytes 835584 | tf_op jit(solution)/shard_map/all_gather | solution.py:30
  85.9 38.7 %while.13 = (s32[]{:T(128)}, f32[12,128,256]{2,0,1:T(8,128)S(1)}, f32[12,128,256]{2,0,1:T(8,128)}, s32[3,8]{1,0:T(4,128)S(1)}, bf16[3,8,128,128]{3,2,1,0:T(8,128...) while((s32[]{:T(128)}, f32[12,128,256]{2,0,1:T(8,128)S(1)}, ...), condition=%wide.region_1.3_spmd.clone, body=%wide.region_0.2_spmd.clone.sunk | while | flops 279972160 | bytes 40903584 | solution.py:55
  85.9 0.0 copy-start.5
  86.0 0.6 gather_fusion
  86.6 0.0 copy-start.2
  86.6 0.2 copy-done.5
  86.8 1.7 gather_fusion.1
  88.5 0.0 copy-start.4
  88.6 0.0 copy-done.2
  88.6 0.8 copy-done.4
  89.3 1.3 fusion.44
  90.7 1.4 fusion.45
  92.1 0.0 copy-start.3
  92.1 0.0 copy-start
  92.1 2.5 select_add_fusion.4
  94.6 0.0 copy-done.3
  94.6 0.4 fusion.46
  95.0 0.0 copy-done
  95.0 0.0 copy-start.6
  95.0 2.5 select_add_fusion.5
  97.5 0.0 copy-start.1
  97.5 1.3 copy-done.1
  98.8 0.0 copy-done.6
  98.9 0.6 gather_fusion
  99.5 0.2 copy-done.5
  99.7 1.7 gather_fusion.1
  101.5 0.8 copy-done.4
  102.2 1.3 fusion.44
  103.6 1.4 fusion.45
  105.0 2.5 select_add_fusion.4
  107.5 0.4 fusion.46
  107.9 2.5 select_add_fusion.5
  110.4 1.3 copy-done.1
  111.8 0.6 gather_fusion
  112.4 0.2 copy-done.5
  112.6 1.7 gather_fusion.1
  114.4 0.8 copy-done.4
  115.1 1.3 fusion.44
  116.5 1.4 fusion.45
  117.9 2.5 select_add_fusion.4
  120.4 0.4 fusion.46
  120.8 2.5 select_add_fusion.5
  123.3 1.3 copy-done.1
  124.6 0.0 copy-done.6
  124.6 3.7 copy.9
  128.3 0.0 all-reduce.7.cloned.1.call-update
  128.3 0.0 all-reduce.5.cloned.1.call-start
  128.4 0.0 copy-start.8
  128.4 0.0 copy-start.7
  128.4 2.1 copy.8
  130.5 0.0 all-reduce.5.cloned.1.call-update
  130.6 23.1 %all-reduce.1 = (f32[256]{0:T(256)S(1)}, f32[256]{0:T(256)S(1)}) all-reduce(f32[256]{0:T(256)S(1)} %convert_reduce_fusion, f32[256]{0:T(256)S(1)} %convert_reduce_fusion.1), channel_id=1, replica_groups=mesh['doc'=16,'gram'=32] {'doc'}, use_global_device_ids=true, to_apply=%region_4.6 | all-reduce | flops 512 | bytes 4096 | tf_op jit(solution)/shard_map/psum | solution.py:66
  153.8 72.3 %all-reduce = (f32[256]{0:T(256)S(1)}, f32[256]{0:T(256)S(1)}) all-reduce(f32[256]{0:T(256)S(1)} %get-tuple-element.103, f32[256]{0:T(256)S(1)} %get-tuple-element.104), channel_id=1, replica_groups=mesh['doc'=16,'gram'=32] {'gram'}, use_global_device_ids=true, to_apply=%region_5.7 | all-reduce | flops 512 | bytes 4096 | tf_op jit(solution)/shard_map/psum | solution.py:66
  226.0 16.6 %all-reduce.7.cloned.1.call-done = f32[1536,256]{1,0:T(8,128)} async-done(((f32[1536,256]{1,0:T(8,128)}), f32[1536,256]{1,0:T(8,128)}) %all-reduce.7.cloned.1.call-update) | async-done | bytes 1572880 | tf_op jit(solution)/shard_map/psum | solution.py:62
  242.7 1.5 fusion.19
  244.2 167.6 %all-reduce.5.cloned.1.call-done = f32[1536,256]{1,0:T(8,128)} async-done(((f32[1536,256]{1,0:T(8,128)}), f32[1536,256]{1,0:T(8,128)}) %all-reduce.5.cloned.1.call-update) | async-done | bytes 1572880 | tf_op jit(solution)/shard_map/psum | solution.py:60
  411.8 1.4 fusion.21
  (46 shorter events, 0.2 us)
Async XLA Ops:
  7.2 235.5 %all-reduce.7.cloned.1.call-start = ((), (), s32[]{:S(2)}) async-start(), calls=%async_computation.1 | async-start | bytes 3145728 | tf_op jit(solution)/shard_map/psum | solution.py:62
  85.9 0.9 copy-start.5
  86.6 2.0 copy-start.2
  88.5 0.8 copy-start.4
  92.1 2.5 copy-start.3
  92.1 2.9 copy-start
  95.0 3.8 copy-start.6
  97.5 1.4 copy-start.1
  98.8 0.9 copy-start.5
  99.5 2.0 copy-start.2
  101.4 0.8 copy-start.4
  105.0 2.5 copy-start.3
  105.0 2.9 copy-start
  107.9 3.8 copy-start.6
  110.4 1.4 copy-start.1
  111.7 0.9 copy-start.5
  112.4 2.0 copy-start.2
  114.3 0.8 copy-start.4
  117.9 2.5 copy-start.3
  117.9 2.9 copy-start
  120.8 3.8 copy-start.6
  123.3 1.4 copy-start.1
  128.3 283.4 %all-reduce.5.cloned.1.call-start = ((), (), s32[]{:S(2)}) async-start(), calls=%async_computation | async-start | bytes 3145728 | tf_op jit(solution)/shard_map/psum | solution.py:60
  128.4 2.2 copy-start.8
  128.4 2.2 copy-start.7
Sparse Core Ops, SparseCore 0:
  128.4 114.1 all-reduce.6
  246.1 165.6 all-reduce.4
